TPU v7x, 512 devices: a whole 4x8x8 slice. The times are simulated.
512 devices in a mesh: samp: 32 (over x, z), blk: 16 (over y, core).
Axes of the slice: x: 4, y: 8, z: 8, core: 2. Of those that a mesh axis runs over, the one named last changes fastest.
Arguments:
- dosages: int32 [49152, 8192], P('samp', 'blk'), may hold values from 0 to 2, as said below
- new_dosages: int32 [49152, 2048], P('samp', 'blk'), may hold values from 0 to 2, as said below
- traits: float32 [64, 49152], P(None, 'samp'), may hold values from -40 to 40
- shrink: float32 [5], replicated, may hold values from 0.5 to 5
Outputs:
- residual: float32 [5, 64, 49152], P(None, 'blk', 'samp')
- scores: float32 [5, 64, 2048], P(None, None, 'blk')
Inputs may be any that keep to these rules, and one draw needn't show every extreme that they name: `dosages`: codes of haplotype pairs, with linkage along neighbouring variants. `new_dosages`: codes of haplotype pairs, with linkage along neighbouring variants.
All inputs are finite; a program needn't handle non-finite values.
Results may differ from a plain program's by a relative error of at most 0.0053.
Values may be sent and summed in bfloat16 or wider, within the bound.
No kernel may reach another device: no remote copies, remote signals or barrier semaphores. Data moves between devices by JAX's collectives and lax.ppermute only.
A program may use at most 64 MiB of HBM per device.

v0:
```python
import jax
import jax.numpy as jnp
from jax import lax
from jax.sharding import Mesh, PartitionSpec as P

RIDGE = 5
SAMP = ("x", "z")
BLK = ("y", "core")
FACTORS = {32: (4, 8), 16: (8, 2), 4: (2, 2)}
EPS = 1e-05
F32 = jnp.float32
BF16 = jnp.bfloat16


def dot(a, b, contract, precision=None):
    return lax.dot_general(
        a, b, (contract, ((), ())), precision=precision, preferred_element_type=F32
    )


def rounded(values):
    return lax.reduce_precision(values, 8, 7)


def column_stats(shifted_sum, shifted_sq, count):
    mean = (shifted_sum + count) / count
    var = (shifted_sq + 2.0 * shifted_sum + count) / count - mean * mean
    return (mean, 1.0 / jnp.sqrt(var + EPS))


def scaled(codes, mean, inv):
    return ((codes.astype(F32) - mean) * inv).astype(BF16)


def affine(shifted_sum, shifted_sq, mean, inv, count):
    low, mid, high = (rounded((code - mean) * inv) for code in (0.0, 1.0, 2.0))
    n_low = (shifted_sq - shifted_sum) * 0.5
    n_high = (shifted_sq + shifted_sum) * 0.5
    n_mid = count - shifted_sq
    value_mean = (n_low * low + n_mid * mid + n_high * high) / count
    pairs = n_low * n_mid + n_mid * n_high + 4.0 * n_low * n_high
    slopes = (
        n_low * n_mid * (mid - low)
        + n_mid * n_high * (high - mid)
        + 2.0 * n_low * n_high * (high - low)
    )
    slope = jnp.where(pairs > 0.0, slopes / jnp.maximum(pairs, 1.0), inv)
    square = (n_low * low * low + n_mid * mid * mid + n_high * high * high) / count
    return (value_mean, slope, square)


def chebyshev_coefficients(lam, bound):
    centre = lam + bound / 2.0
    half = bound / 2.0
    sig = centre / half
    q0 = 1.0 / sig
    d0 = 1.0 / centre
    r1a, r1b = (1.0 - lam * d0, -d0)
    q1 = 1.0 / (2.0 * sig - q0)
    step = 2.0 * q1 / half
    d1a, d1b = (q1 * q0 * d0 + step * r1a, step * r1b)
    r2a = r1a - lam * d1a
    r2b = r1b - d1a - lam * d1b
    r2c = -d1b
    q2 = 1.0 / (2.0 * sig - q1)
    step = 2.0 * q2 / half
    d2a, d2b, d2c = (q2 * q1 * d1a + step * r2a, q2 * q1 * d1b + step * r2b, step * r2c)
    return (d0 + d1a + d2a, d1b + d2b, d2c)


def shards(dosages, new_dosages, traits, shrink):
    rows, width = dosages.shape
    fresh_width = new_dosages.shape[1]
    trait_count = traits.shape[0]
    samp, blk = (lax.axis_size(SAMP), lax.axis_size(BLK))
    depth, cores, zs = (lax.axis_size("y"), lax.axis_size("core"), lax.axis_size("z"))
    count = float(rows * samp)
    half_width = width // 2
    share_rows = half_width // samp
    share = trait_count // blk
    columns = RIDGE * trait_count
    codes = (dosages - 1).astype(BF16)
    codes_f = (dosages - 1).astype(F32)
    new_f = (new_dosages - 1).astype(F32)
    trait_bf = traits.astype(BF16)
    parts = (
        jnp.sum(codes_f, axis=0),
        jnp.sum(codes_f * codes_f, axis=0),
        jnp.sum(new_f, axis=0),
        jnp.sum(new_f * new_f, axis=0),
        jnp.sum(trait_bf.astype(F32), axis=1),
    )
    sizes = [p.shape[0] for p in parts]
    slots = share_rows * 256
    sums = jnp.pad(jnp.concatenate(parts), (0, slots - sum(sizes))).reshape(share_rows, 256)
    first, second = (codes[:, :half_width], codes[:, half_width:])
    over_rows = ((0,), (0,))
    gram_top = dot(first, codes, over_rows)
    gram_low = dot(second, second, over_rows)
    cross = dot(codes, trait_bf, ((0,), (1,)))
    wide = 3 * half_width
    payload = jnp.concatenate(
        [gram_top, gram_low, cross[:half_width], cross[half_width:]], axis=1
    ).reshape(samp, share_rows, wide + 2 * trait_count)
    payload = jnp.concatenate(
        [payload, jnp.broadcast_to(sums[None], (samp, share_rows, 256))], axis=2
    )
    chunk = jnp.sum(lax.all_to_all(payload, SAMP, 0, 0, tiled=True), axis=0)
    totals = chunk[:, wide + 2 * trait_count :].reshape(slots)
    pieces, at = ([], 0)
    for size in sizes:
        pieces.append(totals[at : at + size])
        at += size
    code_sum, code_sq, new_sum, new_sq, trait_sum = pieces
    mean, inv = column_stats(code_sum, code_sq, count)
    value_mean, slope, square = affine(code_sum, code_sq, mean, inv, count)
    start = lax.axis_index(SAMP) * share_rows

    def own(vector, offset):
        return lax.dynamic_slice(vector, (start + offset,), (share_rows,))[:, None]

    def centred(product, offset, column_from):
        sums_i, slope_i, value_i = (own(v, offset) for v in (code_sum, slope, value_mean))
        out = (
            slope_i
            * slope[None, column_from:]
            * (product / count - sums_i / count * (code_sum[None, column_from:] / count))
        )
        out = out + value_i * value_mean[None, column_from:]
        row = start + offset + lax.broadcasted_iota(jnp.int32, out.shape, 0)
        column = column_from + lax.broadcasted_iota(jnp.int32, out.shape, 1)
        return jnp.where(row == column, 0.0, out)

    def centred_cross(product, offset):
        sums_i, slope_i, value_i = (own(v, offset) for v in (code_sum, slope, value_mean))
        trait_mean = trait_sum[None, :] / count
        return slope_i * (product / count - sums_i / count * trait_mean) + value_i * trait_mean

    rhs_rows = jnp.concatenate(
        [
            centred_cross(chunk[:, wide : wide + trait_count], 0),
            centred_cross(chunk[:, wide + trait_count : wide + 2 * trait_count], half_width),
        ],
        axis=1,
    )
    rhs_high = rounded(rhs_rows)
    own_rows = jnp.concatenate(
        [
            centred(chunk[:, :width], 0, 0),
            centred(chunk[:, width:wide], half_width, half_width),
            rhs_high,
            rhs_rows - rhs_high,
        ],
        axis=1,
    ).astype(BF16)
    every = lax.all_to_all(
        jnp.broadcast_to(own_rows[None], (samp, *own_rows.shape)), SAMP, 0, 0, tiled=True
    ).reshape(half_width, own_rows.shape[1])
    top_left, top_right = (every[:, :half_width], every[:, half_width:width])
    low_right = every[:, width:wide]
    gram = jnp.concatenate(
        [
            jnp.concatenate([top_left, top_right], axis=1),
            jnp.concatenate([top_right.T, low_right], axis=1),
        ],
        axis=0,
    )
    bound = jnp.max(jnp.sum(jnp.abs(gram.astype(F32)), axis=0) + square)
    rhs_parts = every[:, wide:].reshape(half_width, 2, 2, trait_count)
    rhs_parts = rhs_parts.transpose(1, 3, 2, 0).reshape(2 * trait_count, width)

    def apply_gram(high, low, whole):
        out = dot(jnp.concatenate([high, low], axis=0), gram, ((1,), (0,)))
        return out[:trait_count] + out[trait_count:] + square[None, :] * whole

    high, low = (rhs_parts[:trait_count], rhs_parts[trait_count:])
    rhs = high.astype(F32) + low.astype(F32)
    once = apply_gram(high, low, rhs)
    once_high = rounded(once)
    twice = apply_gram(once_high.astype(BF16), (once - once_high).astype(BF16), once)
    coefficients = chebyshev_coefficients(shrink, bound)
    row = lax.broadcasted_iota(jnp.int32, (columns, 3 * trait_count), 0)
    column = lax.broadcasted_iota(jnp.int32, (columns, 3 * trait_count), 1)
    side, in_side = (row // (columns // cores), row % (columns // cores))
    place, in_place = (in_side // (RIDGE * share), in_side % (RIDGE * share))
    ridge, in_share = (in_place // share, in_place % share)
    core = lax.rem(lax.axis_index("core") + 1 + side, cores)
    trait = (place * cores + core) * share + in_share
    mixing = jnp.zeros((columns, 3 * trait_count), F32)
    for power in range(3):
        for r in range(RIDGE):
            mixing = jnp.where(
                (ridge == r) & (column == trait + power * trait_count),
                coefficients[power][r],
                mixing,
            )
    weights = dot(
        mixing, jnp.concatenate([rhs, once, twice], axis=0), ((1,), (0,)), lax.Precision.HIGHEST
    ).astype(BF16)
    standard = scaled(dosages, mean, inv)
    new_mean, new_inv = column_stats(new_sum, new_sq, count)
    fresh = scaled(new_dosages, new_mean, new_inv)
    half_columns = columns // cores
    along = ((1,), (1,))
    sent = dot(weights[:half_columns], standard, along).astype(BF16)
    kept = dot(weights[half_columns:], standard, along)
    arrived = lax.ppermute(sent, "core", [(0, 1), (1, 0)])
    paired = (kept + arrived.astype(F32)).astype(BF16).reshape(depth, RIDGE * share, rows)
    summed = lax.all_to_all(paired, "y", 0, 0, tiled=True)
    pred = jnp.sum(summed.astype(F32), axis=0).reshape(RIDGE, share, rows)
    own_traits = lax.dynamic_slice_in_dim(traits, lax.axis_index(BLK) * share, share, 0)
    residual = own_traits[None] - pred
    res_bf = lax.all_gather(
        residual.astype(BF16).reshape(RIDGE * share, rows), BLK, axis=0, tiled=True
    )
    raw_part = dot(res_bf, fresh, ((1,), (0,)))
    res_float = res_bf.astype(F32)
    squares = jnp.sum(res_float * res_float, axis=1).reshape(zs, 1, columns // zs)
    squares = jnp.pad(squares, ((0, 0), (0, 7), (0, fresh_width - columns // zs)))
    ends = jnp.concatenate([raw_part.reshape(zs, columns // zs, fresh_width), squares], axis=1)
    ends = jnp.sum(lax.all_to_all(ends, "z", 0, 0, tiled=True), axis=0)
    ends = lax.psum(ends, "x")
    raw, sum_sq = (ends[: columns // zs], ends[columns // zs, : columns // zs])
    scores = raw / jnp.sqrt(count * (sum_sq / count + EPS))[:, None]
    scores = lax.all_to_all(
        jnp.broadcast_to(scores[None], (zs, *scores.shape)), "z", 0, 0, tiled=True
    )
    scores = scores.reshape(blk, RIDGE, share, fresh_width).transpose(1, 0, 2, 3)
    return (residual, scores.reshape(RIDGE, trait_count, fresh_width))


def solution(mesh):
    samp, blk = (FACTORS[mesh.shape["samp"]], FACTORS[mesh.shape["blk"]])
    grid = Mesh(mesh.devices.reshape(*samp, *blk), SAMP + BLK)
    return jax.shard_map(
        shards,
        mesh=grid,
        in_specs=(P(SAMP, BLK), P(SAMP, BLK), P(None, SAMP), P()),
        out_specs=(P(None, BLK, SAMP), P(None, None, BLK)),
        check_vma=False,
    )
```

profile of v0, /device:TPU:8, one launch (start us, length us, event | category | flops | bytes accessed | tf_op | source)
XLA Modules:
  0.0 220.9 jit_solution(13262179598304185275)
XLA Ops:
  0.6 2.3 %add_convert_fusion = bf16[1536,512]{1,0:T(8,128)(2,1)S(1)} fusion(s32[1536,512]{1,0:T(8,128)} %param.4), kind=kLoop, calls=%fused_computation.3 | loop fusion | flops 1572864 | bytes 4718592 | tf_op jit(solution)/shard_map/convert_element_type | solution.py:82
  3.0 1.4 fusion.2
  4.4 1.1 fusion
  6.6 2.1 fusion.119
  8.8 0.7 fusion.171
  9.8 1.3 constant_dynamic-update-slice_fusion.4
  11.1 1.3 constant_dynamic-update-slice_fusion.3
  12.4 1.3 constant_dynamic-update-slice_fusion.2
  13.6 1.3 constant_dynamic-update-slice_fusion.1
  14.9 1.3 constant_dynamic-update-slice_fusion
  16.2 0.7 pad.8
  16.9 1.4 maximum_bitcast_fusion
  18.3 1.1 pad_maximum_fusion
  19.4 13.3 %all-to-all-start = ((f32[32,8,1152]{2,1,0:T(8,128)}), f32[32,8,1152]{2,1,0:T(8,128)}, u32[]{:S(2)}, u32[]{:S(2)}) async-start(f32[32,8,1152]{2,1,0:T(8,128)} %pad_maximum_fusion), calls=%async_computation | async-start | bytes 2359296 | tf_op jit(solution)/shard_map/all_to_all | solution.py:108
  33.7 30.3 %all-to-all-done = f32[32,8,1152]{2,1,0:T(8,128)} async-done(((f32[32,8,1152]{2,1,0:T(8,128)}), f32[32,8,1152]{2,1,0:T(8,128)}, u32[]{:S(2)}, u32[]{:S(2)}) %all-to-all-start) | async-done | bytes 1179680 | tf_op jit(solution)/shard_map/all_to_all | solution.py:108
  64.0 2.0 reduce_sum.97
  66.0 0.8 slice_bitcast_fusion.1
  67.0 0.7 slice_multiply_fusion.4
  67.7 0.8 fusion.131
  69.1 0.8 fusion.138
  69.9 0.8 fusion.126
  70.8 0.9 broadcast_in_dim.108
  71.6 5.3 %all-to-all-start.1 = ((bf16[32,8,1024]{2,1,0:T(8,128)(2,1)}), bf16[32,8,1024]{2,1,0:T(8,128)(2,1)}, u32[]{:S(2)}, u32[]{:S(2)}) async-start(bf16[32,8,1024]{2,1,0:T(8,128)(2,1)} %broadcast_in_dim.108), calls=%async_computation.1 | async-start | bytes 1048576 | tf_op jit(solution)/shard_map/all_to_all | solution.py:156
  78.7 14.7 %all-to-all-done.1 = bf16[32,8,1024]{2,1,0:T(8,128)(2,1)} async-done(((bf16[32,8,1024]{2,1,0:T(8,128)(2,1)}), bf16[32,8,1024]{2,1,0:T(8,128)(2,1)}, u32[]{:S(2)}, u32[]{:S(2)}) %all-to-all-start.1) | async-done | bytes 524320 | tf_op jit(solution)/shard_map/all_to_all | solution.py:156
  93.5 1.8 fusion.170
  95.3 1.7 concatenate.57
  96.9 1.7 copy.34
  98.6 1.2 abs_reduce_fusion
  100.4 1.4 fusion.150
  105.7 1.7 copy.28
  107.4 0.9 fusion.172
  108.5 1.3 fusion.111
  110.6 11.3 %convolution_convert_fusion.1 = bf16[320,512]{1,0:T(8,128)(2,1)S(1)} fusion(f32[64,512]{1,0:T(8,128)S(1)} %fusion.109, f32[64,512]{1,0:T(8,128)S(1)} %get-tuple-element.14, f32[64,512]{1,0:T(8,128)S(1)} %get-tuple-element.20, f32[]{:T(128)} %bitcast.18, f32[]{:T(128)} %bitcast.17, f32[]{:T(128)} %bitcast.16, f32[]{:T(128)} %bitcast.15, f32[]{:T(128)} %bitcast.14, ...), kind=kOutput, calls=%fused_computation.6 | convolution fusion | flops 383008768 | bytes 726720 | tf_op jit(solution)/shard_map/dot_general | solution.py:16
  121.8 0.7 convolution_convert_fusion
  122.5 1.9 collective-permute-start
  124.5 1.8 collective-permute-done
  126.3 1.5 add_convert_fusion.1
  127.8 2.0 reshape.255
  129.8 7.5 %all-to-all-start.2 = ((bf16[8,20,1536]{2,1,0:T(8,128)(2,1)}), bf16[8,20,1536]{2,1,0:T(8,128)(2,1)S(1)}, u32[]{:S(2)}, u32[]{:S(2)}) async-start(bf16[8,20,1536]{2,1,0:T(8,128)(2,1)} %reshape.255), calls=%async_computation.2 | async-start | bytes 1179648 | tf_op jit(solution)/shard_map/all_to_all | solution.py:209
  137.4 0.8 add_multiply_fusion.4
  138.1 16.9 %all-to-all-done.2 = bf16[8,20,1536]{2,1,0:T(8,128)(2,1)S(1)} async-done(((bf16[8,20,1536]{2,1,0:T(8,128)(2,1)}), bf16[8,20,1536]{2,1,0:T(8,128)(2,1)S(1)}, u32[]{:S(2)}, u32[]{:S(2)}) %all-to-all-start.2) | async-done | bytes 491552 | tf_op jit(solution)/shard_map/all_to_all | solution.py:209
  155.2 19.1 %all-gather = bf16[16,20,1536]{2,1,0:T(8,128)(2,1)S(1)} all-gather(bf16[1,20,1536]{2,1,0:T(8,128)(2,1)S(1)} %fusion.121), channel_id=1, replica_groups=mesh['x'=4,'z'=8,'y'=8,'core'=2] {'y','core'}, dimensions={0}, use_global_device_ids=true | all-gather | bytes 1044480 | tf_op jit(solution)/shard_map/all_gather | solution.py:213
  176.0 4.2 %all-to-all-start.3 = ((f32[8,48,128]{2,1,0:T(8,128)}), f32[8,48,128]{2,1,0:T(8,128)S(1)}, u32[]{:S(2)}, u32[]{:S(2)}) async-start(f32[8,48,128]{2,1,0:T(8,128)} %select_maximum_fusion), calls=%async_computation.3 | async-start | bytes 393216 | tf_op jit(solution)/shard_map/all_to_all | solution.py:221
  180.3 11.0 %all-to-all-done.3 = f32[8,48,128]{2,1,0:T(8,128)S(1)} async-done(((f32[8,48,128]{2,1,0:T(8,128)}), f32[8,48,128]{2,1,0:T(8,128)S(1)}, u32[]{:S(2)}, u32[]{:S(2)}) %all-to-all-start.3) | async-done | bytes 196640 | tf_op jit(solution)/shard_map/all_to_all | solution.py:221
  191.3 15.4 %psum.7 = f32[48,128]{1,0:T(8,128)S(1)} all-reduce(f32[48,128]{1,0:T(8,128)S(1)} %reduce_sum.102), channel_id=1, replica_groups=mesh['x'=4,'z'=8,'y'=8,'core'=2] {'x'}, use_global_device_ids=true, to_apply=%region_11.12 | all-reduce | flops 6144 | bytes 49152 | tf_op jit(solution)/shard_map/psum | solution.py:222
  207.4 3.4 %all-to-all-start.4 = ((f32[8,40,128]{2,1,0:T(8,128)}), f32[8,40,128]{2,1,0:T(8,128)S(1)}, u32[]{:S(2)}, u32[]{:S(2)}) async-start(f32[8,40,128]{2,1,0:T(8,128)} %broadcast_in_dim.125), calls=%async_computation.4 | async-start | bytes 327680 | tf_op jit(solution)/shard_map/all_to_all | solution.py:225
  211.5 8.7 %all-to-all-done.4 = f32[8,40,128]{2,1,0:T(8,128)S(1)} async-done(((f32[8,40,128]{2,1,0:T(8,128)}), f32[8,40,128]{2,1,0:T(8,128)S(1)}, u32[]{:S(2)}, u32[]{:S(2)}) %all-to-all-start.4) | async-done | bytes 163872 | tf_op jit(solution)/shard_map/all_to_all | solution.py:225
  220.2 0.7 copy.31
  (83 shorter events, 13.3 us)
Async XLA Ops:
  3.0 2.5 %copy-start.1 = (bf16[1536,512]{1,0:T(8,128)(2,1)}, bf16[1536,512]{1,0:T(8,128)(2,1)S(1)}, u32[]{:S(2)}) copy-start(bf16[1536,512]{1,0:T(8,128)(2,1)S(1)} %add_convert_fusion) | copy-start | bytes 4718596
  3.0 2.6 %copy-start = (s32[1536,512]{1,0:T(8,128)S(1)}, s32[1536,512]{1,0:T(8,128)}, u32[]{:S(2)}) copy-start(s32[1536,512]{1,0:T(8,128)} %param.4) | copy-start | bytes 9437188
  5.6 1.0 copy-start.4
  6.6 2.9 %copy-start.2 = (s32[1536,128]{1,0:T(8,128)S(1)}, s32[1536,128]{1,0:T(8,128)}, u32[]{:S(2)}) copy-start(s32[1536,128]{1,0:T(8,128)} %param.5) | copy-start | bytes 2359300
  19.4 44.6 %all-to-all-start = ((f32[32,8,1152]{2,1,0:T(8,128)}), f32[32,8,1152]{2,1,0:T(8,128)}, u32[]{:S(2)}, u32[]{:S(2)}) async-start(f32[32,8,1152]{2,1,0:T(8,128)} %pad_maximum_fusion), calls=%async_computation | async-start | bytes 2359296 | tf_op jit(solution)/shard_map/all_to_all | solution.py:108
  68.5 0.6 copy-start.8
  71.6 21.8 %all-to-all-start.1 = ((bf16[32,8,1024]{2,1,0:T(8,128)(2,1)}), bf16[32,8,1024]{2,1,0:T(8,128)(2,1)}, u32[]{:S(2)}, u32[]{:S(2)}) async-start(bf16[32,8,1024]{2,1,0:T(8,128)(2,1)} %broadcast_in_dim.108), calls=%async_computation.1 | async-start | bytes 1048576 | tf_op jit(solution)/shard_map/all_to_all | solution.py:156
  107.4 2.6 %copy-start.5 = (bf16[256,512]{1,0:T(8,128)(2,1)S(1)}, bf16[256,512]{1,0:T(8,128)(2,1)}, u32[]{:S(2)}) copy-start(bf16[256,512]{1,0:T(8,128)(2,1)} %concatenate.57) | copy-start | bytes 786436
  107.4 2.6 %copy-start.6 = (bf16[256,256]{0,1:T(8,128)(2,1)S(1)}, bf16[256,256]{0,1:T(8,128)(2,1)}, u32[]{:S(2)}) copy-start(bf16[256,256]{0,1:T(8,128)(2,1)} %copy.34) | copy-start | bytes 393220
  107.4 2.6 %copy-start.7 = (bf16[256,256]{1,0:T(8,128)(2,1)S(1)}, bf16[256,256]{1,0:T(8,128)(2,1)}, u32[]{:S(2)}) copy-start(bf16[256,256]{1,0:T(8,128)(2,1)} %get-tuple-element.17) | copy-start | bytes 393220
  109.8 0.7 copy-start.9
  109.9 0.7 copy-start.10
  109.9 0.7 copy-start.11
  109.9 0.7 copy-start.12
  109.9 0.7 copy-start.13
  109.9 0.7 copy-start.14
  122.5 3.8 %collective-permute-start = (bf16[160,1536]{1,0:T(8,128)(2,1)S(1)}, bf16[160,1536]{1,0:T(8,128)(2,1)S(1)}, u32[]{:S(2)}, u32[]{:S(2)}) collective-permute-start(bf16[160,1536]{1,0:T(8,128)(2,1)S(1)} %convolution_convert_fusion), channel_id=1, source_target_pairs={{0,1},{1,0},{2,3},{3,2},{4,5},{5,4},{6,7},{7,6},{8,9},{9,8},{10,11... | collective-permute-start | bytes 1474568 | tf_op jit(solution)/shard_map/ppermute | solution.py:207
  129.8 25.3 %all-to-all-start.2 = ((bf16[8,20,1536]{2,1,0:T(8,128)(2,1)}), bf16[8,20,1536]{2,1,0:T(8,128)(2,1)S(1)}, u32[]{:S(2)}, u32[]{:S(2)}) async-start(bf16[8,20,1536]{2,1,0:T(8,128)(2,1)} %reshape.255), calls=%async_computation.2 | async-start | bytes 1179648 | tf_op jit(solution)/shard_map/all_to_all | solution.py:209
  155.2 19.7 %copy-start.3 = (s32[1536,128]{1,0:T(8,128)S(1)}, s32[1536,128]{1,0:T(8,128)}, u32[]{:S(2)}) copy-start(s32[1536,128]{1,0:T(8,128)} %param.5) | copy-start | bytes 2359300
  176.0 15.2 %all-to-all-start.3 = ((f32[8,48,128]{2,1,0:T(8,128)}), f32[8,48,128]{2,1,0:T(8,128)S(1)}, u32[]{:S(2)}, u32[]{:S(2)}) async-start(f32[8,48,128]{2,1,0:T(8,128)} %select_maximum_fusion), calls=%async_computation.3 | async-start | bytes 393216 | tf_op jit(solution)/shard_map/all_to_all | solution.py:221
  207.4 12.7 %all-to-all-start.4 = ((f32[8,40,128]{2,1,0:T(8,128)}), f32[8,40,128]{2,1,0:T(8,128)S(1)}, u32[]{:S(2)}, u32[]{:S(2)}) async-start(f32[8,40,128]{2,1,0:T(8,128)} %broadcast_in_dim.125), calls=%async_computation.4 | async-start | bytes 327680 | tf_op jit(solution)/shard_map/all_to_all | solution.py:225
where the time goes:
time: 223 us; the launch traced here: 221 us
  waiting for transfers between devices  83.4 us (37%)
  starting transfers between devices  35.7 us (16%)
  blocking collectives  34.5 us (15%)
  local copies, waits for them, and re-layouts  25.3 us (11%)
  other arithmetic  20.5 us (9%)
  matrix products  20 us (9%)
    all_to_all x1, waiting for transfers between devices, shards(): chunk = jnp.sum(lax.all_to_all(payload, SAMP, 0, 0, tiled=True), axis=0)  30.3 us
    dot_general x9, matrix products, dot(): lax.dot_general(a, b, (contract, ((), ())), precision=precision, preferre...  20 us
    all_gather x1, blocking collectives, shards(): lax.all_gather(residual.astype(BF16).reshape(RIDGE * share, rows), BLK, a...  19.1 us
    all_to_all x1, waiting for transfers between devices, shards(): summed = lax.all_to_all(paired, 'y', 0, 0, tiled=True)  16.9 us
    psum x1, blocking collectives, shards(): ends = lax.psum(ends, 'x')  15.4 us
    all_to_all x1, waiting for transfers between devices, shards(): lax.all_to_all(jnp.broadcast_to(own_rows[None], (samp, *own_rows.shape)),...  14.7 us
    all_to_all x1, starting transfers between devices, shards(): chunk = jnp.sum(lax.all_to_all(payload, SAMP, 0, 0, tiled=True), axis=0)  13.3 us
    all_to_all x1, waiting for transfers between devices, shards(): ends = jnp.sum(lax.all_to_all(ends, 'z', 0, 0, tiled=True), axis=0)  11 us
  transfers between devices with their start and end apart: 6, of which 6 were waited for; matrix products, arithmetic and copies ran while one was open for 2% of the time, Pallas kernels for 0%

commit v1 on v0

--- a/solution.py
+++ b/solution.py
@@ -210,8 +210,14 @@
     pred = jnp.sum(summed.astype(F32), axis=0).reshape(RIDGE, share, rows)
     own_traits = lax.dynamic_slice_in_dim(traits, lax.axis_index(BLK) * share, share, 0)
     residual = own_traits[None] - pred
-    res_bf = lax.all_gather(
-        residual.astype(BF16).reshape(RIDGE * share, rows), BLK, axis=0, tiled=True
+    res_bf = jnp.concatenate(
+        lax.all_to_all(
+            jnp.stack([residual.astype(BF16).reshape(RIDGE * share, rows)] * lax.axis_size(BLK)),
+            BLK,
+            0,
+            0,
+        ),
+        axis=0,
     )
     raw_part = dot(res_bf, fresh, ((1,), (0,)))
     res_float = res_bf.astype(F32)

time: 223 us -> 238 us (1.067)
  the two profiles are of different devices: /device:TPU:8 before, /device:TPU:24 now
where the time goes in v1:
time: 238 us; the launch traced here: 236 us
  waiting for transfers between devices  109 us (46%)
  starting transfers between devices  43.3 us (18%)
  local copies, waits for them, and re-layouts  25.7 us (11%)
  other arithmetic  20.6 us (9%)
  matrix products  20 us (8%)
  blocking collectives  15.4 us (6%)
    all_to_all x1, waiting for transfers between devices, shards(): chunk = jnp.sum(lax.all_to_all(payload, SAMP, 0, 0, tiled=True), axis=0)  30.2 us
    all_to_all x1, waiting for transfers between devices, shards(): lax.all_to_all(jnp.stack([residual.astype(BF16).reshape(RIDGE * share, ro...  28.3 us
    dot_general x9, matrix products, dot(): lax.dot_general(a, b, (contract, ((), ())), precision=precision, preferre...  20 us
    psum x1, blocking collectives, shards(): ends = lax.psum(ends, 'x')  15.4 us
    all_to_all x1, waiting for transfers between devices, shards(): summed = lax.all_to_all(paired, 'y', 0, 0, tiled=True)  14.9 us
    all_to_all x1, waiting for transfers between devices, shards(): lax.all_to_all(jnp.broadcast_to(own_rows[None], (samp, *own_rows.shape)),...  14.8 us
    all_to_all x1, starting transfers between devices, shards(): chunk = jnp.sum(lax.all_to_all(payload, SAMP, 0, 0, tiled=True), axis=0)  13.3 us
    all_to_all x1, waiting for transfers between devices, shards(): ends = jnp.sum(lax.all_to_all(ends, 'z', 0, 0, tiled=True), axis=0)  10.7 us
  transfers between devices with their start and end apart: 7, of which 7 were waited for; matrix products, arithmetic and copies ran while one was open for 2% of the time, Pallas kernels for 0%

profile of v1, /device:TPU:24, one launch (start us, length us, event | category | flops | bytes accessed | tf_op | source)
XLA Modules:
  0.0 236.1 jit_solution(4615177918906513351)
XLA Ops:
  0.6 2.3 add_convert_fusion
  3.0 1.4 fusion.2
  4.4 1.1 fusion
  6.2 2.1 fusion.121
  8.4 0.7 fusion.172
  9.4 1.3 constant_dynamic-update-slice_fusion.4
  10.6 1.3 constant_dynamic-update-slice_fusion.3
  11.9 1.3 constant_dynamic-update-slice_fusion.2
  13.2 1.3 constant_dynamic-update-slice_fusion.1
  14.5 1.3 constant_dynamic-update-slice_fusion
  16.5 1.4 maximum_bitcast_fusion
  17.9 1.1 pad_maximum_fusion
  19.0 13.3 %all-to-all-start = ((f32[32,8,1152]{2,1,0:T(8,128)}), f32[32,8,1152]{2,1,0:T(8,128)}, u32[]{:S(2)}, u32[]{:S(2)}) async-start(f32[32,8,1152]{2,1,0:T(8,128)} %pad_maximum_fusion), calls=%async_computation | async-start | bytes 2359296 | tf_op jit(solution)/shard_map/all_to_all | solution.py:108
  33.4 30.2 %all-to-all-done = f32[32,8,1152]{2,1,0:T(8,128)} async-done(((f32[32,8,1152]{2,1,0:T(8,128)}), f32[32,8,1152]{2,1,0:T(8,128)}, u32[]{:S(2)}, u32[]{:S(2)}) %all-to-all-start) | async-done | bytes 1179680 | tf_op jit(solution)/shard_map/all_to_all | solution.py:108
  63.6 2.0 reduce_sum.97
  65.6 0.8 slice_bitcast_fusion.1
  66.5 0.7 slice_multiply_fusion.4
  67.2 0.8 fusion.132
  68.6 0.8 fusion.139
  69.5 0.8 fusion.127
  70.4 0.9 broadcast_in_dim.108
  71.2 5.3 %all-to-all-start.1 = ((bf16[32,8,1024]{2,1,0:T(8,128)(2,1)}), bf16[32,8,1024]{2,1,0:T(8,128)(2,1)}, u32[]{:S(2)}, u32[]{:S(2)}) async-start(bf16[32,8,1024]{2,1,0:T(8,128)(2,1)} %broadcast_in_dim.108), calls=%async_computation.1 | async-start | bytes 1048576 | tf_op jit(solution)/shard_map/all_to_all | solution.py:156
  78.3 14.8 %all-to-all-done.1 = bf16[32,8,1024]{2,1,0:T(8,128)(2,1)} async-done(((bf16[32,8,1024]{2,1,0:T(8,128)(2,1)}), bf16[32,8,1024]{2,1,0:T(8,128)(2,1)}, u32[]{:S(2)}, u32[]{:S(2)}) %all-to-all-start.1) | async-done | bytes 524320 | tf_op jit(solution)/shard_map/all_to_all | solution.py:156
  93.1 1.8 fusion.171
  94.8 1.7 concatenate.57
  96.5 1.7 copy.26
  98.2 1.2 abs_reduce_fusion
  100.0 1.5 fusion.151
  105.5 1.7 copy.20
  107.1 0.9 fusion.173
  108.3 1.3 fusion.113
  110.1 11.3 %convolution_convert_fusion.1 = bf16[320,512]{1,0:T(8,128)(2,1)S(1)} fusion(f32[64,512]{1,0:T(8,128)S(1)} %fusion.111, f32[64,512]{1,0:T(8,128)S(1)} %get-tuple-element.14, f32[64,512]{1,0:T(8,128)S(1)} %get-tuple-element.20, f32[]{:T(128)} %bitcast.18, f32[]{:T(128)} %bitcast.17, f32[]{:T(128)} %bitcast.16, f32[]{:T(128)} %bitcast.15, f32[]{:T(128)} %bitcast.14, ...), kind=kOutput, calls=%fused_computation.6 | convolution fusion | flops 383008768 | bytes 726720 | tf_op jit(solution)/shard_map/dot_general | solution.py:16
  122.1 1.9 collective-permute-start
  124.0 1.8 collective-permute-done
  125.8 1.5 add_convert_fusion.1
  127.3 2.0 reshape.260
  129.3 7.3 %all-to-all-start.2 = ((bf16[8,20,1536]{2,1,0:T(8,128)(2,1)}), bf16[8,20,1536]{2,1,0:T(8,128)(2,1)S(1)}, u32[]{:S(2)}, u32[]{:S(2)}) async-start(bf16[8,20,1536]{2,1,0:T(8,128)(2,1)} %reshape.260), calls=%async_computation.2 | async-start | bytes 1179648 | tf_op jit(solution)/shard_map/all_to_all | solution.py:209
  136.7 14.9 %all-to-all-done.2 = bf16[8,20,1536]{2,1,0:T(8,128)(2,1)S(1)} async-done(((bf16[8,20,1536]{2,1,0:T(8,128)(2,1)}), bf16[8,20,1536]{2,1,0:T(8,128)(2,1)S(1)}, u32[]{:S(2)}, u32[]{:S(2)}) %all-to-all-start.2) | async-done | bytes 491552 | tf_op jit(solution)/shard_map/all_to_all | solution.py:209
  151.7 1.1 stack.3
  152.8 7.9 %all-to-all-start.3 = ((bf16[16,20,1536]{2,1,0:T(8,128)(2,1)}), bf16[16,20,1536]{2,1,0:T(8,128)(2,1)S(1)}, u32[]{:S(2)}, u32[]{:S(2)}) async-start(bf16[16,20,1536]{2,1,0:T(8,128)(2,1)} %stack.3), calls=%async_computation.3 | async-start | bytes 2359296 | tf_op jit(solution)/shard_map/all_to_all | solution.py:214
  160.7 0.8 add_multiply_fusion.4
  161.5 28.3 %all-to-all-done.3 = bf16[16,20,1536]{2,1,0:T(8,128)(2,1)S(1)} async-done(((bf16[16,20,1536]{2,1,0:T(8,128)(2,1)}), bf16[16,20,1536]{2,1,0:T(8,128)(2,1)S(1)}, u32[]{:S(2)}, u32[]{:S(2)}) %all-to-all-start.3) | async-done | bytes 983072 | tf_op jit(solution)/shard_map/all_to_all | solution.py:214
  190.8 0.7 select_maximum_fusion
  191.5 4.2 %all-to-all-start.4 = ((f32[8,48,128]{2,1,0:T(8,128)}), f32[8,48,128]{2,1,0:T(8,128)S(1)}, u32[]{:S(2)}, u32[]{:S(2)}) async-start(f32[8,48,128]{2,1,0:T(8,128)} %select_maximum_fusion), calls=%async_computation.4 | async-start | bytes 393216 | tf_op jit(solution)/shard_map/all_to_all | solution.py:227
  195.8 10.7 %all-to-all-done.4 = f32[8,48,128]{2,1,0:T(8,128)S(1)} async-done(((f32[8,48,128]{2,1,0:T(8,128)}), f32[8,48,128]{2,1,0:T(8,128)S(1)}, u32[]{:S(2)}, u32[]{:S(2)}) %all-to-all-start.4) | async-done | bytes 196640 | tf_op jit(solution)/shard_map/all_to_all | solution.py:227
  206.5 15.4 %psum.7 = f32[48,128]{1,0:T(8,128)S(1)} all-reduce(f32[48,128]{1,0:T(8,128)S(1)} %reduce_sum.102), channel_id=1, replica_groups=mesh['x'=4,'z'=8,'y'=8,'core'=2] {'x'}, use_global_device_ids=true, to_apply=%region_11.12 | all-reduce | flops 6144 | bytes 49152 | tf_op jit(solution)/shard_map/psum | solution.py:228
  222.7 3.4 %all-to-all-start.5 = ((f32[8,40,128]{2,1,0:T(8,128)}), f32[8,40,128]{2,1,0:T(8,128)S(1)}, u32[]{:S(2)}, u32[]{:S(2)}) async-start(f32[8,40,128]{2,1,0:T(8,128)} %broadcast_in_dim.125), calls=%async_computation.5 | async-start | bytes 327680 | tf_op jit(solution)/shard_map/all_to_all | solution.py:231
  226.8 8.7 %all-to-all-done.5 = f32[8,40,128]{2,1,0:T(8,128)S(1)} async-done(((f32[8,40,128]{2,1,0:T(8,128)}), f32[8,40,128]{2,1,0:T(8,128)S(1)}, u32[]{:S(2)}, u32[]{:S(2)}) %all-to-all-start.5) | async-done | bytes 163872 | tf_op jit(solution)/shard_map/all_to_all | solution.py:231
  (85 shorter events, 14.1 us)
Async XLA Ops:
  3.0 2.5 %copy-start.1 = (bf16[1536,512]{1,0:T(8,128)(2,1)}, bf16[1536,512]{1,0:T(8,128)(2,1)S(1)}, u32[]{:S(2)}) copy-start(bf16[1536,512]{1,0:T(8,128)(2,1)S(1)} %add_convert_fusion) | copy-start | bytes 4718596
  3.0 2.6 %copy-start = (s32[1536,512]{1,0:T(8,128)S(1)}, s32[1536,512]{1,0:T(8,128)}, u32[]{:S(2)}) copy-start(s32[1536,512]{1,0:T(8,128)} %param.4) | copy-start | bytes 9437188
  4.4 1.8 copy-start.4
  6.2 2.9 %copy-start.2 = (s32[1536,128]{1,0:T(8,128)S(1)}, s32[1536,128]{1,0:T(8,128)}, u32[]{:S(2)}) copy-start(s32[1536,128]{1,0:T(8,128)} %param.5) | copy-start | bytes 2359300
  19.0 44.6 %all-to-all-start = ((f32[32,8,1152]{2,1,0:T(8,128)}), f32[32,8,1152]{2,1,0:T(8,128)}, u32[]{:S(2)}, u32[]{:S(2)}) async-start(f32[32,8,1152]{2,1,0:T(8,128)} %pad_maximum_fusion), calls=%async_computation | async-start | bytes 2359296 | tf_op jit(solution)/shard_map/all_to_all | solution.py:108
  68.0 0.6 copy-start.8
  71.2 21.8 %all-to-all-start.1 = ((bf16[32,8,1024]{2,1,0:T(8,128)(2,1)}), bf16[32,8,1024]{2,1,0:T(8,128)(2,1)}, u32[]{:S(2)}, u32[]{:S(2)}) async-start(bf16[32,8,1024]{2,1,0:T(8,128)(2,1)} %broadcast_in_dim.108), calls=%async_computation.1 | async-start | bytes 1048576 | tf_op jit(solution)/shard_map/all_to_all | solution.py:156
  107.1 2.6 %copy-start.5 = (bf16[256,512]{1,0:T(8,128)(2,1)S(1)}, bf16[256,512]{1,0:T(8,128)(2,1)}, u32[]{:S(2)}) copy-start(bf16[256,512]{1,0:T(8,128)(2,1)} %concatenate.57) | copy-start | bytes 786436
  107.1 2.6 %copy-start.6 = (bf16[256,256]{0,1:T(8,128)(2,1)S(1)}, bf16[256,256]{0,1:T(8,128)(2,1)}, u32[]{:S(2)}) copy-start(bf16[256,256]{0,1:T(8,128)(2,1)} %copy.26) | copy-start | bytes 393220
  107.1 2.6 %copy-start.7 = (bf16[256,256]{1,0:T(8,128)(2,1)S(1)}, bf16[256,256]{1,0:T(8,128)(2,1)}, u32[]{:S(2)}) copy-start(bf16[256,256]{1,0:T(8,128)(2,1)} %get-tuple-element.17) | copy-start | bytes 393220
  108.3 1.8 copy-start.9
  108.3 1.8 copy-start.10
  108.3 1.8 copy-start.11
  108.3 1.8 copy-start.12
  108.3 1.8 copy-start.13
  108.3 1.8 copy-start.14
  122.1 3.8 %collective-permute-start = (bf16[160,1536]{1,0:T(8,128)(2,1)S(1)}, bf16[160,1536]{1,0:T(8,128)(2,1)S(1)}, u32[]{:S(2)}, u32[]{:S(2)}) collective-permute-start(bf16[160,1536]{1,0:T(8,128)(2,1)S(1)} %convolution_convert_fusion), channel_id=1, source_target_pairs={{0,1},{1,0},{2,3},{3,2},{4,5},{5,4},{6,7},{7,6},{8,9},{9,8},{10,11... | collective-permute-start | bytes 1474568 | tf_op jit(solution)/shard_map/ppermute | solution.py:207
  129.3 22.3 %all-to-all-start.2 = ((bf16[8,20,1536]{2,1,0:T(8,128)(2,1)}), bf16[8,20,1536]{2,1,0:T(8,128)(2,1)S(1)}, u32[]{:S(2)}, u32[]{:S(2)}) async-start(bf16[8,20,1536]{2,1,0:T(8,128)(2,1)} %reshape.260), calls=%async_computation.2 | async-start | bytes 1179648 | tf_op jit(solution)/shard_map/all_to_all | solution.py:209
  152.8 37.5 %copy-start.3 = (s32[1536,128]{1,0:T(8,128)S(1)}, s32[1536,128]{1,0:T(8,128)}, u32[]{:S(2)}) copy-start(s32[1536,128]{1,0:T(8,128)} %param.5) | copy-start | bytes 2359300
  152.8 36.9 %all-to-all-start.3 = ((bf16[16,20,1536]{2,1,0:T(8,128)(2,1)}), bf16[16,20,1536]{2,1,0:T(8,128)(2,1)S(1)}, u32[]{:S(2)}, u32[]{:S(2)}) async-start(bf16[16,20,1536]{2,1,0:T(8,128)(2,1)} %stack.3), calls=%async_computation.3 | async-start | bytes 2359296 | tf_op jit(solution)/shard_map/all_to_all | solution.py:214
  191.5 15.0 %all-to-all-start.4 = ((f32[8,48,128]{2,1,0:T(8,128)}), f32[8,48,128]{2,1,0:T(8,128)S(1)}, u32[]{:S(2)}, u32[]{:S(2)}) async-start(f32[8,48,128]{2,1,0:T(8,128)} %select_maximum_fusion), calls=%async_computation.4 | async-start | bytes 393216 | tf_op jit(solution)/shard_map/all_to_all | solution.py:227
  222.7 12.7 %all-to-all-start.5 = ((f32[8,40,128]{2,1,0:T(8,128)}), f32[8,40,128]{2,1,0:T(8,128)S(1)}, u32[]{:S(2)}, u32[]{:S(2)}) async-start(f32[8,40,128]{2,1,0:T(8,128)} %broadcast_in_dim.125), calls=%async_computation.5 | async-start | bytes 327680 | tf_op jit(solution)/shard_map/all_to_all | solution.py:231
